TPU v7x, 32 devices: a whole 2x2x4 slice. The times are simulated.
32 devices in a mesh: sub: 8 (over z, x), scen: 4 (over y, core).
Axes of the slice: x: 2, y: 2, z: 4, core: 2. Of those that a mesh axis runs over, the one named last changes fastest.
Arguments:
- internal_inverse: bfloat16 [32, 1024, 1024], P('sub', 'scen')
- schur_inverse: bfloat16 [512, 512], P('sub')
- port_nodes: int32 [32, 16], P('sub'), may hold values from 0 to 1023, as said below
- turbine_count: int32 [8], P('sub'), may hold values from 1 to 4, as said below
- partner_port: int32 [512], P('sub'), may hold values from 0 to 511, as said below
- cable_delay: int32 [512], P('sub'), may hold values from 2 to 4, as said below
- history_w: bfloat16 [4, 256, 512], P(None, 'scen', 'sub'), may hold values from -6 to 6
- node_state: float32 [256, 32, 1024], P('scen', 'sub'), may hold values from -6 to 6
- node_gain: float32 [32, 1024], P('sub'), may hold values from 0.02 to 0.3
- stroke_node: int32 [256], P('scen'), may hold values from 0 to 32767, as said below
- stroke_amp: float32 [256], P('scen'), may hold values from 3 to 30
Outputs:
- node_voltage: bfloat16 [256, 32, 1024], P('scen', 'sub')
- cable_waves: bfloat16 [3, 256, 512], P(None, 'scen', 'sub')
Inputs may be any that keep to these rules, and one draw needn't show every extreme that they name: `port_nodes`: the 16 nodes named for one slot are distinct. `turbine_count`: the turbines of one index of sub fill its first slots; the busiest hold all 4. `partner_port`: a cable joins two ports that name each other, of a turbine and the next turbine in slot order (the next used slot, on the same or the next index of sub); a port that names itself has no cable. `cable_delay`: both ends of a cable carry the same delay. `stroke_node`: slot times 1024 plus local node; a stroke on an empty slot injects nothing.
All inputs are finite; a program needn't handle non-finite values.
Results may differ from a plain program's by a relative error of at most 0.004.
The roundings to bfloat16 on the way count: a program that leaves them out, or rounds other values in their place, can miss the bound.
Values may be sent and summed in bfloat16 or wider, within the bound.
A program may use at most 64 MiB of HBM per device.

v0:
```python
import math
import jax
import jax.numpy as jnp
from jax import lax
from jax.sharding import PartitionSpec as P

STEPS = 3


def padded(block, sides, width):
    for axis, dim in sides:
        count = lax.axis_size(axis)
        forward = [(i, i + 1) for i in range(count - 1)]
        backward = [(target, source) for source, target in forward]
        low = lax.ppermute(
            lax.slice_in_dim(block, block.shape[dim] - width, None, axis=dim), axis, forward
        )
        high = lax.ppermute(lax.slice_in_dim(block, 0, width, axis=dim), axis, backward)
        block = jnp.concatenate([low, block, high], axis=dim)
    return block


def per_device(
    internal_inverse,
    schur_inverse,
    port_nodes,
    turbine_count,
    partner_port,
    cable_delay,
    history_w,
    node_state,
    node_gain,
    stroke_node,
    stroke_amp,
):
    slot_count = port_nodes.shape[0]
    port_count = port_nodes.shape[1]
    node_count = internal_inverse.shape[2]
    scen_rows = node_state.shape[0]
    depth = history_w.shape[0]
    if_dev = slot_count * port_count
    device = lax.axis_index("sub")
    slot_used = (jnp.arange(slot_count, dtype=jnp.int32) < turbine_count[0]).astype(jnp.float32)
    port_used = jnp.repeat(slot_used, port_count)
    node_range = jnp.arange(node_count, dtype=jnp.int32)
    port_hot = (port_nodes[:, :, None] == node_range[None, None, :]).astype(jnp.float32)
    node_ids = (device * slot_count + jnp.arange(slot_count, dtype=jnp.int32))[
        :, None
    ] * node_count + node_range[None, :]
    stroke_hot = (stroke_node[:, None, None] == node_ids[None]).astype(jnp.float32)
    own_ports = device * if_dev + jnp.arange(if_dev, dtype=jnp.int32)
    paired = (partner_port != own_ports).astype(jnp.float32)
    partner_col = partner_port - (device - 1) * if_dev
    history_wide = padded(history_w, (("sub", 2),), if_dev)
    hist_cols = jnp.take(history_wide, partner_col, axis=2).astype(jnp.float32)
    schur_wide = schur_inverse.astype(jnp.float32)
    full_inverse = lax.all_gather(internal_inverse, "scen", axis=1, tiled=True)
    port_rows = jnp.take_along_axis(full_inverse, port_nodes[:, :, None], axis=1)
    fresh_cols = jnp.zeros((scen_rows, if_dev), jnp.float32)
    companion = node_state
    wave_list = []
    voltage = jnp.zeros((scen_rows, slot_count, node_count), jnp.float32)
    for step_index in range(STEPS):
        time_now = step_index + 1
        lag_time = time_now - cable_delay
        picked = jnp.zeros((scen_rows, if_dev), jnp.float32)
        for delay_back in range(depth):
            picked = picked + jnp.where(
                (lag_time == -delay_back)[None, :], hist_cols[delay_back], 0.0
            )
        picked = picked + jnp.where((lag_time == 1)[None, :], fresh_cols, 0.0)
        cable_in = -picked * paired[None, :]
        inject = jnp.einsum(
            "sgp,gpn->sgn",
            cable_in.reshape(scen_rows, slot_count, port_count),
            port_hot,
            precision=lax.Precision.HIGHEST,
        )
        wave_value = math.exp(-0.3 * time_now) - math.exp(-2.0 * time_now)
        strike = (stroke_amp * wave_value)[:, None, None] * stroke_hot
        injected = (slot_used[None, :, None] * (companion + strike + inject)).astype(jnp.bfloat16)
        opened = jnp.einsum(
            "sgm,gmn->sgn", injected, full_inverse, preferred_element_type=jnp.float32
        )
        port_open = jnp.take_along_axis(opened, port_nodes[None], axis=2).reshape(scen_rows, if_dev)
        every_port = lax.all_gather(port_open, "sub", axis=1, tiled=True)
        link_current = lax.dot_general(
            every_port,
            schur_wide,
            (((1,), (1,)), ((), ())),
            precision=lax.Precision.HIGHEST,
            preferred_element_type=jnp.float32,
        )
        link_half = link_current.astype(jnp.bfloat16).reshape(scen_rows, slot_count, port_count)
        correction = jnp.einsum(
            "sgp,gpn->sgn", link_half, port_rows, preferred_element_type=jnp.float32
        )
        voltage = slot_used[None, :, None] * (opened - correction)
        companion = -companion - 2.0 * node_gain[None] * voltage
        port_volt = jnp.take_along_axis(voltage, port_nodes[None], axis=2).reshape(
            scen_rows, if_dev
        )
        outgoing = (port_used[None, :] * (0.5 * port_volt + cable_in)).astype(jnp.bfloat16)
        wave_list.append(outgoing)
        if step_index == 0:
            fresh_wide = padded(outgoing, (("sub", 1),), if_dev)
            fresh_cols = jnp.take(fresh_wide, partner_col, axis=1).astype(jnp.float32)
    return (voltage.astype(jnp.bfloat16), jnp.stack(wave_list))


def solution(mesh):
    return jax.shard_map(
        per_device,
        mesh=mesh,
        in_specs=(
            P("sub", "scen", None),
            P("sub", None),
            P("sub", None),
            P("sub"),
            P("sub"),
            P("sub"),
            P(None, "scen", "sub"),
            P("scen", "sub", None),
            P("sub", None),
            P("scen"),
            P("scen"),
        ),
        out_specs=(P("scen", "sub", None), P(None, "scen", "sub")),
        check_vma=False,
    )
```

profile of v0, /device:TPU:0, one launch (start us, length us, event | category | flops | bytes accessed | tf_op | source)
XLA Modules:
  0.0 228.1 jit_solution(14548788545594329199)
XLA Ops:
  7.3 0.7 all-gather.2.cloned.1.call-update
  8.1 0.1 copy.44
  8.2 4.8 %collective-permute-start = (bf16[4,64,64]{1,0,2:T(4,128)(2,1)S(1)}, bf16[4,64,64]{1,0,2:T(4,128)(2,1)S(1)}, u32[]{:S(2)}, u32[]{:S(2)}) collective-permute-start(bf16[4,64,64]{1,0,2:T(4,128)(2,1)S(1)} %copy.44), channel_id=1, source_target_pairs={{0,4},{4,8},{8,12},{12,16},{16,20},{20,24},{24,28},{1,5},{5,9},{9,... | collective-permute-start | bytes 98312 | tf_op jit(solution)/shard_map/ppermute | solution.py:15
  13.0 1.3 collective-permute-start.1
  15.2 0.6 broadcast_multiply_fusion.1
  16.0 0.6 broadcast_multiply_fusion
  17.0 0.1 reshape.565
  17.2 0.6 mul.248
  17.9 0.6 broadcast_in_dim.277
  18.5 0.6 broadcast_in_dim.267
  19.1 0.6 broadcast_in_dim.269
  19.6 0.7 broadcast_in_dim.271
  20.3 0.6 broadcast_in_dim.273
  20.9 0.6 broadcast_in_dim.275
  21.5 0.7 broadcast_in_dim.286
  22.2 0.6 broadcast_in_dim.288
  22.8 0.6 broadcast_in_dim.290
  23.4 0.6 broadcast_in_dim.292
  24.0 0.7 broadcast_in_dim.294
  24.7 0.2 pad_maximum_fusion
  24.9 0.7 gather_fusion
  25.6 0.1 convert_bitcast_fusion
  25.7 0.1 fusion.99
  25.9 1.3 fusion.12
  27.2 43.5 %all-gather.2.cloned.1.call-done = bf16[4,1024,1024]{2,1,0:T(8,128)(2,1)} async-done(((bf16[4,256,1024]{2,1,0:T(8,128)(2,1)}), bf16[4,1024,1024]{2,1,0:T(8,128)(2,1)}) %all-gather.2.cloned.1.call-update) | async-done | bytes 8388624 | tf_op jit(solution)/shard_map/all_gather | solution.py:57
  70.7 5.0 %convolution_bitcast_fusion.7 = f32[64,4,1024]{2,0,1:T(8,128)S(1)} fusion(bf16[64,4,1024]{2,0,1:T(8,128)(2,1)S(1)} %fusion.12, bf16[4,1024,1024]{2,1,0:T(8,128)(2,1)} %all-gather.2.cloned.1.call-done), kind=kOutput, calls=%fused_computation.29 | convolution fusion | flops 536870912 | bytes 9961472 | tf_op jit(solution)/shard_map/sgm,gmn->sgn/dot_general | solution.py:82
  75.8 1.9 copy.47
  77.8 1.5 gather_fusion.3
  79.3 30.8 %all_gather.13 = f32[64,512]{0,1:T(8,128)S(1)} all-gather(f32[64,64]{0,1:T(8,128)S(1)} %bitcast.170), channel_id=1, replica_groups=mesh['sub'=8,'scen'=4] {'sub'}, dimensions={1}, use_global_device_ids=true | all-gather | bytes 147456 | tf_op jit(solution)/shard_map/all_gather | solution.py:86
  110.1 0.4 convolution_convert_fusion.2
  110.5 0.1 copy.48
  110.6 1.8 gather_fusion.2
  112.4 0.4 fusion.9
  112.8 0.6 copy.49
  113.4 0.9 gather_fusion.4
  114.3 0.9 fusion.45
  115.3 3.4 %collective-permute-start.2 = (bf16[64,64]{0,1:T(8,128)(2,1)S(1)}, bf16[64,64]{0,1:T(8,128)(2,1)S(1)}, u32[]{:S(2)}, u32[]{:S(2)}) collective-permute-start(bf16[64,64]{0,1:T(8,128)(2,1)S(1)} %fusion.45), channel_id=1, source_target_pairs={{0,4},{4,8},{8,12},{12,16},{16,20},{20,24},{24,28},{1,5},{5,9},{9,... | collective-permute-start | bytes 24584 | tf_op jit(solution)/shard_map/ppermute | solution.py:15
  118.6 1.3 collective-permute-start.3
  119.9 2.0 multiply_convert_fusion.2
  121.9 2.3 %collective-permute-done.3 = bf16[64,64]{0,1:T(8,128)(2,1)S(1)} collective-permute-done((bf16[64,64]{0,1:T(8,128)(2,1)S(1)}, bf16[64,64]{0,1:T(8,128)(2,1)S(1)}, u32[]{:S(2)}, u32[]{:S(2)}) %collective-permute-start.3) | collective-permute-done | bytes 8224 | tf_op jit(solution)/shard_map/ppermute | solution.py:18
  124.3 0.8 gather_fusion.1
  125.0 2.8 %fusion.13 = bf16[64,4,1024]{2,0,1:T(8,128)(2,1)S(1)} fusion(f32[64]{0:T(128)} %get-tuple-element.35, s32[4,1024]{1,0:T(4,128)} %copy-done.14, f32[4]{0:T(128)} %copy-done.21, s32[64]{0:T(128)} %param.22, f32[64,4,1024]{2,0,1:T(8,128)S(1)} %fusion.9, f32[4,1024]{1,0:T(4,128)} %broadcast_multiply_fusion, f32[64,4,1024]{2,1,0:T(4,128)} %param.20, ...), kind=kOutput, calls=%fused_computation.34 | convolution fusion | flops 52809728 | bytes 2729360 | tf_op jit(solution)/shard_map/sgp,gpn->sgn/dot_general | solution.py:73
  127.8 5.0 %convolution_bitcast_fusion.4 = f32[64,4,1024]{2,0,1:T(8,128)S(1)} fusion(bf16[64,4,1024]{2,0,1:T(8,128)(2,1)S(1)} %fusion.13, bf16[4,1024,1024]{2,1,0:T(8,128)(2,1)} %all-gather.2.cloned.1.call-done), kind=kOutput, calls=%fused_computation.22 | convolution fusion | flops 536870912 | bytes 9961472 | tf_op jit(solution)/shard_map/sgm,gmn->sgn/dot_general | solution.py:82
  132.8 1.9 copy.50
  134.8 1.5 gather_fusion.5
  136.3 30.9 %all_gather.14 = f32[64,512]{0,1:T(8,128)S(1)} all-gather(f32[64,64]{0,1:T(8,128)S(1)} %bitcast.171), channel_id=1, replica_groups=mesh['sub'=8,'scen'=4] {'sub'}, dimensions={1}, use_global_device_ids=true | all-gather | bytes 147456 | tf_op jit(solution)/shard_map/all_gather | solution.py:86
  167.2 0.4 convolution_convert_fusion.1
  167.7 1.0 fusion.5
  168.9 1.9 copy.54
  171.0 2.8 %fusion.14 = bf16[64,4,1024]{2,0,1:T(8,128)(2,1)S(1)} fusion(f32[64,4,1024]{2,0,1:T(8,128)S(1)} %fusion.5, f32[64]{0:T(128)S(1)} %copy-done.35, s32[4,1024]{1,0:T(4,128)S(1)} %copy-done.15, f32[4,1024]{1,0:T(4,128)S(1)} %copy-done.16, f32[4]{0:T(128)S(1)} %copy-done.22, s32[64]{0:T(128)S(1)} %copy-done.57, f32[64,4,1024]{2,0,1:T(8,128)S(1)} %fusion.9, ...), kind=kOutput, calls=%fused_computation.35 | convolution fusion | flops 53596160 | bytes 3777936 | tf_op jit(solution)/shard_map/sgp,gpn->sgn/dot_general | solution.py:73
  173.7 5.0 %convolution_bitcast_fusion.1 = f32[64,4,1024]{2,0,1:T(8,128)S(1)} fusion(bf16[64,4,1024]{2,0,1:T(8,128)(2,1)S(1)} %fusion.14, bf16[4,1024,1024]{2,1,0:T(8,128)(2,1)} %all-gather.2.cloned.1.call-done), kind=kOutput, calls=%fused_computation.15 | convolution fusion | flops 536870912 | bytes 9961472 | tf_op jit(solution)/shard_map/sgm,gmn->sgn/dot_general | solution.py:82
  178.7 0.6 copy.52
  179.4 0.9 gather_fusion.6
  180.3 30.7 %all_gather.15 = f32[64,512]{0,1:T(8,128)S(1)} all-gather(f32[64,64]{0,1:T(8,128)S(1)} %bitcast.172), channel_id=1, replica_groups=mesh['sub'=8,'scen'=4] {'sub'}, dimensions={1}, use_global_device_ids=true | all-gather | bytes 147456 | tf_op jit(solution)/shard_map/all_gather | solution.py:86
  211.0 0.4 convolution_convert_fusion
  211.5 1.2 fusion.100
  212.8 1.9 copy.57
  214.7 1.5 gather_fusion.8
  216.2 0.9 gather_fusion.7
  217.3 0.9 multiply_convert_fusion.1
  218.3 0.9 multiply_convert_fusion
  219.2 0.1 pad_maximum_fusion.1
  219.4 0.7 copy.59
  220.1 1.2 copy.58
  (161 shorter events, 1.7 us)
Async XLA Ops:
  7.2 103.0 %copy-start = (bf16[64,512]{1,0:T(8,128)(2,1)S(1)}, bf16[64,512]{1,0:T(8,128)(2,1)}, u32[]{:S(2)}) copy-start(bf16[64,512]{1,0:T(8,128)(2,1)} %param.14) | copy-start | bytes 196612
  7.2 7.8 %copy-start.65 = (s32[64]{0:T(128)S(1)}, s32[64]{0:T(128)}, u32[]{:S(2)}) copy-start(s32[64]{0:T(128)} %param.17) | copy-start | bytes 772
  7.2 7.8 %copy-start.66 = (s32[64]{0:T(128)S(1)}, s32[64]{0:T(128)}, u32[]{:S(2)}) copy-start(s32[64]{0:T(128)} %param.18) | copy-start | bytes 772
  7.2 8.0 %copy-start.64 = (f32[64]{0:T(128)S(1)}, f32[64]{0:T(128)}, u32[]{:S(2)}) copy-start(f32[64]{0:T(128)} %param.23) | copy-start | bytes 772
  7.2 8.6 %copy-start.18 = (s32[4,16]{1,0:T(4,128)S(1)}, s32[4,16]{1,0:T(4,128)}, u32[]{:S(2)}) copy-start(s32[4,16]{1,0:T(4,128)} %param.15) | copy-start | bytes 772
  7.2 8.7 %copy-start.19 = (f32[4,1024]{1,0:T(4,128)S(1)}, f32[4,1024]{1,0:T(4,128)}, u32[]{:S(2)}) copy-start(f32[4,1024]{1,0:T(4,128)} %param.21) | copy-start | bytes 49156
  7.2 18.6 %copy-start.3 = (f32[64,4,1024]{2,1,0:T(4,128)S(1)}, f32[64,4,1024]{2,1,0:T(4,128)}, u32[]{:S(2)}) copy-start(f32[64,4,1024]{2,1,0:T(4,128)} %param.20) | copy-start | bytes 3145732
  7.3 18.6 %copy-start.56 = (s32[64]{0:T(128)S(1)}, s32[64]{0:T(128)}, u32[]{:S(2)}) copy-start(s32[64]{0:T(128)} %param.22) | copy-start | bytes 772
  7.3 63.4 %all-gather.2.cloned.1.call-start = ((), (), s32[]{:S(2)}) async-start(), calls=%async_computation | async-start | bytes 10485760 | tf_op jit(solution)/shard_map/all_gather | solution.py:57
  8.2 16.5 %collective-permute-start = (bf16[4,64,64]{1,0,2:T(4,128)(2,1)S(1)}, bf16[4,64,64]{1,0,2:T(4,128)(2,1)S(1)}, u32[]{:S(2)}, u32[]{:S(2)}) collective-permute-start(bf16[4,64,64]{1,0,2:T(4,128)(2,1)S(1)} %copy.44), channel_id=1, source_target_pairs={{0,4},{4,8},{8,12},{12,16},{16,20},{20,24},{24,28},{1,5},{5,9},{9,... | collective-permute-start | bytes 98312 | tf_op jit(solution)/shard_map/ppermute | solution.py:15
  13.0 11.7 %collective-permute-start.1 = (bf16[4,64,64]{1,0,2:T(4,128)(2,1)S(1)}, bf16[4,64,64]{1,0,2:T(4,128)(2,1)S(1)}, u32[]{:S(2)}, u32[]{:S(2)}) collective-permute-start(bf16[4,64,64]{1,0,2:T(4,128)(2,1)S(1)} %copy.44), channel_id=1, source_target_pairs={{4,0},{8,4},{12,8},{16,12},{20,16},{24,20},{28,24},{5,1},{9,5},{13... | collective-permute-start | bytes 98312 | tf_op jit(solution)/shard_map/ppermute | solution.py:18
  15.1 10.5 %copy-start.40 = (pred[64]{0:T(512)(128)(4,1)}, pred[64]{0:T(512)(128)(4,1)S(1)}, u32[]{:S(2)}) copy-start(pred[64]{0:T(512)(128)(4,1)S(1)} %get-tuple-element.50) | copy-start | bytes 196
  15.1 10.5 %copy-start.42 = (pred[64]{0:T(512)(128)(4,1)}, pred[64]{0:T(512)(128)(4,1)S(1)}, u32[]{:S(2)}) copy-start(pred[64]{0:T(512)(128)(4,1)S(1)} %get-tuple-element.51) | copy-start | bytes 196
  15.1 10.5 %copy-start.44 = (pred[64]{0:T(512)(128)(4,1)}, pred[64]{0:T(512)(128)(4,1)S(1)}, u32[]{:S(2)}) copy-start(pred[64]{0:T(512)(128)(4,1)S(1)} %get-tuple-element.52) | copy-start | bytes 196
  15.1 10.5 %copy-start.46 = (pred[64]{0:T(512)(128)(4,1)}, pred[64]{0:T(512)(128)(4,1)S(1)}, u32[]{:S(2)}) copy-start(pred[64]{0:T(512)(128)(4,1)S(1)} %get-tuple-element.39) | copy-start | bytes 196
  15.1 10.5 %copy-start.48 = (pred[64]{0:T(512)(128)(4,1)}, pred[64]{0:T(512)(128)(4,1)S(1)}, u32[]{:S(2)}) copy-start(pred[64]{0:T(512)(128)(4,1)S(1)} %get-tuple-element.44) | copy-start | bytes 196
  15.1 10.5 %copy-start.50 = (pred[64]{0:T(512)(128)(4,1)}, pred[64]{0:T(512)(128)(4,1)S(1)}, u32[]{:S(2)}) copy-start(pred[64]{0:T(512)(128)(4,1)S(1)} %get-tuple-element.45) | copy-start | bytes 196
  15.1 10.5 %copy-start.52 = (pred[64]{0:T(512)(128)(4,1)}, pred[64]{0:T(512)(128)(4,1)S(1)}, u32[]{:S(2)}) copy-start(pred[64]{0:T(512)(128)(4,1)S(1)} %get-tuple-element.46) | copy-start | bytes 196
  15.1 10.5 %copy-start.54 = (pred[64]{0:T(512)(128)(4,1)}, pred[64]{0:T(512)(128)(4,1)S(1)}, u32[]{:S(2)}) copy-start(pred[64]{0:T(512)(128)(4,1)S(1)} %get-tuple-element.47) | copy-start | bytes 196
  15.1 60.6 %copy-start.24 = (pred[64]{0:T(512)(128)(4,1)}, pred[64]{0:T(512)(128)(4,1)S(1)}, u32[]{:S(2)}) copy-start(pred[64]{0:T(512)(128)(4,1)S(1)} %get-tuple-element.9) | copy-start | bytes 196
  15.1 60.6 %copy-start.32 = (pred[64]{0:T(512)(128)(4,1)}, pred[64]{0:T(512)(128)(4,1)S(1)}, u32[]{:S(2)}) copy-start(pred[64]{0:T(512)(128)(4,1)S(1)} %get-tuple-element.41) | copy-start | bytes 196
  15.2 60.6 %copy-start.33 = (pred[64]{0:T(512)(128)(4,1)}, pred[64]{0:T(512)(128)(4,1)S(1)}, u32[]{:S(2)}) copy-start(pred[64]{0:T(512)(128)(4,1)S(1)} %get-tuple-element.42) | copy-start | bytes 196
  15.2 60.6 %copy-start.34 = (pred[64]{0:T(512)(128)(4,1)}, pred[64]{0:T(512)(128)(4,1)S(1)}, u32[]{:S(2)}) copy-start(pred[64]{0:T(512)(128)(4,1)S(1)} %get-tuple-element.43) | copy-start | bytes 196
  15.2 60.6 %copy-start.36 = (pred[64]{0:T(512)(128)(4,1)}, pred[64]{0:T(512)(128)(4,1)S(1)}, u32[]{:S(2)}) copy-start(pred[64]{0:T(512)(128)(4,1)S(1)} %get-tuple-element.48) | copy-start | bytes 196
  15.2 60.6 %copy-start.38 = (pred[64]{0:T(512)(128)(4,1)}, pred[64]{0:T(512)(128)(4,1)S(1)}, u32[]{:S(2)}) copy-start(pred[64]{0:T(512)(128)(4,1)S(1)} %get-tuple-element.49) | copy-start | bytes 196
  15.2 60.5 %copy-start.30 = (s32[1024]{0:T(1024)}, s32[1024]{0:T(1024)S(1)}, u32[]{:S(2)}) copy-start(s32[1024]{0:T(1024)S(1)} %pad_clamp_fusion) | copy-start | bytes 12292
  15.9 96.5 %copy-start.28 = (pred[4,16]{1,0:T(4,128)(4,1)}, pred[4,16]{1,0:T(4,128)(4,1)S(1)}, u32[]{:S(2)}) copy-start(pred[4,16]{1,0:T(4,128)(4,1)S(1)} %compare_and_fusion) | copy-start | bytes 196
  16.0 59.8 %copy-start.14 = (s32[4,1024]{1,0:T(4,128)}, s32[4,1024]{1,0:T(4,128)S(1)}, u32[]{:S(2)}) copy-start(s32[4,1024]{1,0:T(4,128)S(1)} %iota_add_fusion) | copy-start | bytes 49156
  16.6 95.8 %copy-start.21 = (f32[4]{0:T(128)}, f32[4]{0:T(128)S(1)}, u32[]{:S(2)}) copy-start(f32[4]{0:T(128)S(1)} %compare_convert_fusion.1) | copy-start | bytes 52
  16.6 59.1 %copy-start.26 = (f32[4,16]{1,0:T(4,128)}, f32[4,16]{1,0:T(4,128)S(1)}, u32[]{:S(2)}) copy-start(f32[4,16]{1,0:T(4,128)S(1)} %mul.238) | copy-start | bytes 772
  25.8 50.0 %copy-start.4 = (f32[1,64,64]{1,0,2:T(1,128)}, f32[1,64,64]{1,0,2:T(1,128)S(1)}, u32[]{:S(2)}) copy-start(f32[1,64,64]{1,0,2:T(1,128)S(1)} %get-tuple-element.12) | copy-start | bytes 49156
  25.9 50.0 %copy-start.6 = (f32[1,64,64]{1,0,2:T(1,128)}, f32[1,64,64]{1,0,2:T(1,128)S(1)}, u32[]{:S(2)}) copy-start(f32[1,64,64]{1,0,2:T(1,128)S(1)} %get-tuple-element.13) | copy-start | bytes 49156
  25.9 49.9 %copy-start.8 = (f32[1,64,64]{1,0,2:T(1,128)}, f32[1,64,64]{1,0,2:T(1,128)S(1)}, u32[]{:S(2)}) copy-start(f32[1,64,64]{1,0,2:T(1,128)S(1)} %get-tuple-element.14) | copy-start | bytes 49156
  115.3 6.7 %collective-permute-start.2 = (bf16[64,64]{0,1:T(8,128)(2,1)S(1)}, bf16[64,64]{0,1:T(8,128)(2,1)S(1)}, u32[]{:S(2)}, u32[]{:S(2)}) collective-permute-start(bf16[64,64]{0,1:T(8,128)(2,1)S(1)} %fusion.45), channel_id=1, source_target_pairs={{0,4},{4,8},{8,12},{12,16},{16,20},{20,24},{24,28},{1,5},{5,9},{9,... | collective-permute-start | bytes 24584 | tf_op jit(solution)/shard_map/ppermute | solution.py:15
  118.6 5.6 %collective-permute-start.3 = (bf16[64,64]{0,1:T(8,128)(2,1)S(1)}, bf16[64,64]{0,1:T(8,128)(2,1)S(1)}, u32[]{:S(2)}, u32[]{:S(2)}) collective-permute-start(bf16[64,64]{0,1:T(8,128)(2,1)S(1)} %fusion.45), channel_id=1, source_target_pairs={{4,0},{8,4},{12,8},{16,12},{20,16},{24,20},{28,24},{5,1},{9,5},{13... | collective-permute-start | bytes 24584 | tf_op jit(solution)/shard_map/ppermute | solution.py:18
  125.0 7.8 %copy-start.10 = (bf16[64,64]{1,0:T(8,128)(2,1)}, bf16[64,64]{1,0:T(8,128)(2,1)S(1)}, u32[]{:S(2)}) copy-start(bf16[64,64]{1,0:T(8,128)(2,1)S(1)} %gather_fusion.1) | copy-start | bytes 24580
  168.7 2.1 copy-start.5
  168.7 2.1 copy-start.7
  168.7 2.1 copy-start.9
  168.8 2.1 copy-start.11
  168.8 2.1 copy-start.15
  168.8 2.1 copy-start.16
  168.8 2.1 copy-start.22
  168.8 2.1 copy-start.27
  168.8 2.1 copy-start.35
  168.8 2.1 copy-start.57
  178.7 32.8 %copy-start.23 = (f32[4]{0:T(128)S(1)}, f32[4]{0:T(128)}, u32[]{:S(2)}) copy-start(f32[4]{0:T(128)} %copy-done.21) | copy-start | bytes 52
  178.7 32.8 %copy-start.29 = (pred[4,16]{1,0:T(4,128)(4,1)S(1)}, pred[4,16]{1,0:T(4,128)(4,1)}, u32[]{:S(2)}) copy-start(pred[4,16]{1,0:T(4,128)(4,1)} %copy-done.28) | copy-start | bytes 196
  212.7 3.5 %copy-start.1 = (f32[64,4,1024]{0,2,1:T(8,128)S(1)}, f32[64,4,1024]{0,2,1:T(8,128)}, u32[]{:S(2)}) copy-start(f32[64,4,1024]{0,2,1:T(8,128)} %copy.54) | copy-start | bytes 3145732
  212.7 4.5 %copy-start.12 = (bf16[64,64]{1,0:T(8,128)(2,1)S(1)}, bf16[64,64]{1,0:T(8,128)(2,1)}, u32[]{:S(2)}) copy-start(bf16[64,64]{1,0:T(8,128)(2,1)} %copy-done.10) | copy-start | bytes 24580
  212.7 4.5 %copy-start.20 = (f32[64]{0:T(128)S(1)}, f32[64]{0:T(128)}, u32[]{:S(2)}) copy-start(f32[64]{0:T(128)} %mul.248) | copy-start | bytes 772
  212.7 4.5 %copy-start.25 = (pred[64]{0:T(512)(128)(4,1)S(1)}, pred[64]{0:T(512)(128)(4,1)}, u32[]{:S(2)}) copy-start(pred[64]{0:T(512)(128)(4,1)} %copy-done.24) | copy-start | bytes 196
  212.7 4.5 %copy-start.47 = (pred[64]{0:T(512)(128)(4,1)S(1)}, pred[64]{0:T(512)(128)(4,1)}, u32[]{:S(2)}) copy-start(pred[64]{0:T(512)(128)(4,1)} %copy-done.46) | copy-start | bytes 196
  212.7 4.5 %copy-start.49 = (pred[64]{0:T(512)(128)(4,1)S(1)}, pred[64]{0:T(512)(128)(4,1)}, u32[]{:S(2)}) copy-start(pred[64]{0:T(512)(128)(4,1)} %copy-done.48) | copy-start | bytes 196
  212.7 4.5 %copy-start.51 = (pred[64]{0:T(512)(128)(4,1)S(1)}, pred[64]{0:T(512)(128)(4,1)}, u32[]{:S(2)}) copy-start(pred[64]{0:T(512)(128)(4,1)} %copy-done.50) | copy-start | bytes 196
  212.7 4.5 %copy-start.53 = (pred[64]{0:T(512)(128)(4,1)S(1)}, pred[64]{0:T(512)(128)(4,1)}, u32[]{:S(2)}) copy-start(pred[64]{0:T(512)(128)(4,1)} %copy-done.52) | copy-start | bytes 196
  212.7 4.5 %copy-start.55 = (pred[64]{0:T(512)(128)(4,1)S(1)}, pred[64]{0:T(512)(128)(4,1)}, u32[]{:S(2)}) copy-start(pred[64]{0:T(512)(128)(4,1)} %copy-done.54) | copy-start | bytes 196
  214.7 3.5 %copy-start.37 = (pred[64]{0:T(512)(128)(4,1)S(1)}, pred[64]{0:T(512)(128)(4,1)}, u32[]{:S(2)}) copy-start(pred[64]{0:T(512)(128)(4,1)} %copy-done.36) | copy-start | bytes 196
  214.7 3.5 %copy-start.39 = (pred[64]{0:T(512)(128)(4,1)S(1)}, pred[64]{0:T(512)(128)(4,1)}, u32[]{:S(2)}) copy-start(pred[64]{0:T(512)(128)(4,1)} %copy-done.38) | copy-start | bytes 196
  214.7 3.5 %copy-start.41 = (pred[64]{0:T(512)(128)(4,1)S(1)}, pred[64]{0:T(512)(128)(4,1)}, u32[]{:S(2)}) copy-start(pred[64]{0:T(512)(128)(4,1)} %copy-done.40) | copy-start | bytes 196
  214.7 3.6 %copy-start.43 = (pred[64]{0:T(512)(128)(4,1)S(1)}, pred[64]{0:T(512)(128)(4,1)}, u32[]{:S(2)}) copy-start(pred[64]{0:T(512)(128)(4,1)} %copy-done.42) | copy-start | bytes 196
  214.7 3.6 %copy-start.45 = (pred[64]{0:T(512)(128)(4,1)S(1)}, pred[64]{0:T(512)(128)(4,1)}, u32[]{:S(2)}) copy-start(pred[64]{0:T(512)(128)(4,1)} %copy-done.44) | copy-start | bytes 196
  214.7 4.5 %copy-start.13 = (bf16[1,64,64]{1,0,2:T(2,128)(2,1)S(1)}, bf16[1,64,64]{1,0,2:T(2,128)(2,1)}, u32[]{:S(2)}) copy-start(bf16[1,64,64]{1,0,2:T(2,128)(2,1)} %multiply_convert_fusion.2) | copy-start | bytes 24580
  214.7 5.4 %copy-start.2 = (bf16[64,4,1024]{2,0,1:T(8,128)(2,1)S(1)}, bf16[64,4,1024]{2,0,1:T(8,128)(2,1)}, u32[]{:S(2)}) copy-start(bf16[64,4,1024]{2,0,1:T(8,128)(2,1)} %get-tuple-element.37) | copy-start | bytes 1572868
  (8 other events, 15.2 us)
Sparse Core Ops, SparseCore 0:
  9.7 60.9 all-gather.1
where the time goes:
time: 229 us; the launch traced here: 228 us
  blocking collectives  92.5 us (40%)
  waiting for transfers between devices  46.5 us (20%)
  local copies, waits for them, and re-layouts  30 us (13%)
  matrix products  25.5 us (11%)
  between operations  15.8 us (7%)
  starting transfers between devices  10.8 us (5%)
  other arithmetic  6.98 us (3%)
    all_gather x3, blocking collectives, per_device(): every_port = lax.all_gather(port_open, 'sub', axis=1, tiled=True)  92.5 us
    all_gather x1, waiting for transfers between devices, per_device(): full_inverse = lax.all_gather(internal_inverse, 'scen', axis=1, tiled=True)  43.5 us
    dot_general x3, matrix products, per_device(): jnp.einsum('sgm,gmn->sgn', injected, full_inverse, preferred_element_type...  15 us
    ppermute x2, starting transfers between devices, padded(): lax.ppermute(lax.slice_in_dim(block, block.shape[dim] - width, None, axis...  8.21 us
    dot_general x3, matrix products, per_device(): jnp.einsum('sgp,gpn->sgn', cable_in.reshape(scen_rows, slot_count, port_c...  6.85 us
    broadcast_in_dim x12, local copies, waits for them, and re-layouts, per_device(): jnp.where((lag_time == -delay_back)[None, :], hist_cols[delay_back], 0.0)  5.29 us
    convert_element_type x4, other arithmetic, per_device(): (port_used[None, :] * (0.5 * port_volt + cable_in)).astype(jnp.bfloat16)  4.8 us
  transfers between devices with their start and end apart: 5, of which 2 were waited for; matrix products, arithmetic and copies ran while one was open for 6% of the time, Pallas kernels for 0%

commit v1 on v0

--- a/solution.py
+++ b/solution.py
@@ -83,7 +83,16 @@
             "sgm,gmn->sgn", injected, full_inverse, preferred_element_type=jnp.float32
         )
         port_open = jnp.take_along_axis(opened, port_nodes[None], axis=2).reshape(scen_rows, if_dev)
-        every_port = lax.all_gather(port_open, "sub", axis=1, tiled=True)
+        val, r_now = (lax.axis_size("sub"), lax.axis_index("sub"))
+        every_port, vec_out = (port_open, 1)
+        while vec_out < val:
+            block_last = lax.ppermute(
+                every_port, "sub", tuple(((m, m ^ vec_out) for m in range(val)))
+            )
+            w1 = jnp.concatenate([every_port, block_last], 1)
+            row_out = jnp.concatenate([block_last, every_port], 1)
+            every_port = jnp.where(r_now & vec_out == 0, w1, row_out)
+            vec_out = 2 * vec_out
         link_current = lax.dot_general(
             every_port,
             schur_wide,

time: 229 us -> 183 us (0.80)
  blocking collectives: 92.5 us -> 0 us
  waiting for transfers between devices: 46.5 us -> 69.6 us
  starting transfers between devices: 10.8 us -> 31.6 us
    all_gather x3 -> x0, blocking collectives: 92.5 us -> none  [per_device(): every_port = lax.all_gather(port_open, 'sub', axis=1, tiled=True)]
    ppermute x0 -> x9, starting transfers between devices: none -> 20.5 us  [per_device(): lax.ppermute(every_port, 'sub', tuple(((m, m ^ vec_out) for m in range(va...]
    ppermute x0 -> x9, waiting for transfers between devices: none -> 17.6 us  [per_device(): lax.ppermute(every_port, 'sub', tuple(((m, m ^ vec_out) for m in range(va...]
    all_gather x1, waiting for transfers between devices: 43.5 us -> 49 us  [per_device(): full_inverse = lax.all_gather(internal_inverse, 'scen', axis=1, tiled=True)]
  transfers between devices with their start and end apart: 5 -> 14, of which waited for: 2 -> 10; matrix products, arithmetic and copies ran while one was open for 6% -> 10% of each run, Pallas kernels for 0% -> 0%
where the time goes in v1:
time: 183 us; the launch traced here: 182 us
  waiting for transfers between devices  69.6 us (38%)
  local copies, waits for them, and re-layouts  31.8 us (17%)
  starting transfers between devices  31.6 us (17%)
  matrix products  25.6 us (14%)
  between operations  15.6 us (9%)
  other arithmetic  8 us (4%)
    all_gather x1, waiting for transfers between devices, per_device(): full_inverse = lax.all_gather(internal_inverse, 'scen', axis=1, tiled=True)  49 us
    ppermute x9, starting transfers between devices, per_device(): lax.ppermute(every_port, 'sub', tuple(((m, m ^ vec_out) for m in range(va...  20.5 us
    ppermute x9, waiting for transfers between devices, per_device(): lax.ppermute(every_port, 'sub', tuple(((m, m ^ vec_out) for m in range(va...  17.6 us
    dot_general x3, matrix products, per_device(): jnp.einsum('sgm,gmn->sgn', injected, full_inverse, preferred_element_type...  15 us
    ppermute x2, starting transfers between devices, padded(): lax.ppermute(lax.slice_in_dim(block, block.shape[dim] - width, None, axis...  8.22 us
    dot_general x3, matrix products, per_device(): jnp.einsum('sgp,gpn->sgn', cable_in.reshape(scen_rows, slot_count, port_c...  6.89 us
    transpose x3, local copies, waits for them, and re-layouts, per_device(): jnp.einsum('sgm,gmn->sgn', injected, full_inverse, preferred_element_type...  5.76 us
    broadcast_in_dim x12, local copies, waits for them, and re-layouts, per_device(): jnp.where((lag_time == -delay_back)[None, :], hist_cols[delay_back], 0.0)  5.63 us
  transfers between devices with their start and end apart: 14, of which 10 were waited for; matrix products, arithmetic and copies ran while one was open for 10% of the time, Pallas kernels for 0%

profile of v1, /device:TPU:0, one launch (start us, length us, event | category | flops | bytes accessed | tf_op | source)
XLA Modules:
  0.0 182.1 jit_solution(15889680045200923253)
XLA Ops:
  7.3 0.7 all-gather.2.cloned.1.call-update
  8.2 4.8 %collective-permute-start = (bf16[4,64,64]{1,0,2:T(4,128)(2,1)S(1)}, bf16[4,64,64]{1,0,2:T(4,128)(2,1)S(1)}, u32[]{:S(2)}, u32[]{:S(2)}) collective-permute-start(bf16[4,64,64]{1,0,2:T(4,128)(2,1)S(1)} %copy.44), channel_id=1, source_target_pairs={{0,4},{4,8},{8,12},{12,16},{16,20},{20,24},{24,28},{1,5},{5,9},{9,... | collective-permute-start | bytes 98312 | tf_op jit(solution)/shard_map/ppermute | solution.py:15
  13.0 1.3 collective-permute-start.1
  15.0 0.6 compare_and_fusion.1
  16.9 2.3 %collective-permute-done.1 = bf16[4,64,64]{1,0,2:T(4,128)(2,1)S(1)} collective-permute-done((bf16[4,64,64]{1,0,2:T(4,128)(2,1)S(1)}, bf16[4,64,64]{1,0,2:T(4,128)(2,1)S(1)}, u32[]{:S(2)}, u32[]{:S(2)}) %collective-permute-start.1) | collective-permute-done | bytes 32800 | tf_op jit(solution)/shard_map/ppermute | solution.py:18
  19.4 0.7 gather_fusion
  20.3 1.3 fusion.12
  21.6 49.0 %all-gather.2.cloned.1.call-done = bf16[4,1024,1024]{2,1,0:T(8,128)(2,1)} async-done(((bf16[4,256,1024]{2,1,0:T(8,128)(2,1)}), bf16[4,1024,1024]{2,1,0:T(8,128)(2,1)}) %all-gather.2.cloned.1.call-update) | async-done | bytes 8388624 | tf_op jit(solution)/shard_map/all_gather | solution.py:57
  70.7 5.0 %convolution_bitcast_fusion.7 = f32[64,4,1024]{2,0,1:T(8,128)S(1)} fusion(bf16[64,4,1024]{2,0,1:T(8,128)(2,1)S(1)} %fusion.12, bf16[4,1024,1024]{2,1,0:T(8,128)(2,1)} %all-gather.2.cloned.1.call-done), kind=kOutput, calls=%fused_computation.29 | convolution fusion | flops 536870912 | bytes 9961472 | tf_op jit(solution)/shard_map/sgm,gmn->sgn/dot_general | solution.py:82
  75.8 1.9 %copy.47 = f32[64,4,1024]{0,2,1:T(8,128)} copy(f32[64,4,1024]{2,0,1:T(8,128)S(1)} %convolution_bitcast_fusion.7) | data formatting | bytes 2097152 | tf_op jit(solution)/shard_map/sgm,gmn->sgn/transpose | solution.py:82
  77.7 1.5 gather_fusion.3
  79.3 1.5 collective-permute-start.2
  80.8 2.4 %collective-permute-done.2 = f32[64,64]{0,1:T(8,128)S(1)} collective-permute-done((f32[64,64]{0,1:T(8,128)S(1)}, f32[64,64]{0,1:T(8,128)S(1)}, u32[]{:S(2)}, u32[]{:S(2)}) %collective-permute-start.2) | collective-permute-done | bytes 16416 | tf_op jit(solution)/shard_map/ppermute | solution.py:89
  83.2 1.6 collective-permute-start.3
  84.8 2.8 %collective-permute-done.3 = f32[64,128]{0,1:T(8,128)S(1)} collective-permute-done((f32[64,128]{0,1:T(8,128)S(1)}, f32[64,128]{0,1:T(8,128)S(1)}, u32[]{:S(2)}, u32[]{:S(2)}) %collective-permute-start.3) | collective-permute-done | bytes 32800 | tf_op jit(solution)/shard_map/ppermute | solution.py:89
  87.6 2.5 %collective-permute-start.4 = (f32[64,256]{0,1:T(8,128)S(1)}, f32[64,256]{0,1:T(8,128)S(1)}, u32[]{:S(2)}, u32[]{:S(2)}) collective-permute-start(f32[64,256]{0,1:T(8,128)S(1)} %maximum_select_fusion.6), channel_id=1, source_target_pairs={{0,16},{4,20},{8,24},{12,28},{16,0},{20,4},{24,8},{28,12},{1,17},{... | collective-permute-start | bytes 196616 | tf_op jit(solution)/shard_map/ppermute | solution.py:89
  90.2 0.6 mul.248
  90.8 1.8 gather_fusion.2
  92.6 2.3 %collective-permute-done.4 = f32[64,256]{0,1:T(8,128)S(1)} collective-permute-done((f32[64,256]{0,1:T(8,128)S(1)}, f32[64,256]{0,1:T(8,128)S(1)}, u32[]{:S(2)}, u32[]{:S(2)}) %collective-permute-start.4) | collective-permute-done | bytes 65568 | tf_op jit(solution)/shard_map/ppermute | solution.py:89
  96.4 0.9 gather_fusion.4
  97.4 0.9 fusion.63
  98.3 3.4 %collective-permute-start.5 = (bf16[64,64]{0,1:T(8,128)(2,1)S(1)}, bf16[64,64]{0,1:T(8,128)(2,1)S(1)}, u32[]{:S(2)}, u32[]{:S(2)}) collective-permute-start(bf16[64,64]{0,1:T(8,128)(2,1)S(1)} %fusion.63), channel_id=1, source_target_pairs={{0,4},{4,8},{8,12},{12,16},{16,20},{20,24},{24,28},{1,5},{5,9},{9,... | collective-permute-start | bytes 24584 | tf_op jit(solution)/shard_map/ppermute | solution.py:15
  101.7 1.5 collective-permute-start.6
  103.2 0.7 broadcast_multiply_fusion
  103.9 0.7 broadcast_in_dim.277
  104.6 0.7 broadcast_in_dim.267
  105.3 0.7 broadcast_in_dim.269
  106.0 0.7 broadcast_in_dim.271
  106.7 0.7 broadcast_in_dim.273
  107.4 0.7 broadcast_in_dim.275
  108.1 0.8 gather_fusion.1
  108.9 2.8 %fusion.13 = bf16[64,4,1024]{2,0,1:T(8,128)(2,1)S(1)} fusion(f32[64]{0:T(128)} %get-tuple-element.35, s32[4,1024]{1,0:T(4,128)} %copy-done.12, f32[4]{0:T(128)} %copy-done.18, s32[64]{0:T(128)} %param.22, f32[64,4,1024]{2,0,1:T(8,128)S(1)} %fusion.9, f32[4,1024]{1,0:T(4,128)S(1)} %broadcast_multiply_fusion, f32[64,4,1024]{2,1,0:T(4,128)} %param.20, ...), kind=kOutput, calls=%fused_computation.34 | convolution fusion | flops 52809728 | bytes 2729360 | tf_op jit(solution)/shard_map/sgp,gpn->sgn/dot_general | solution.py:73
  111.6 5.0 %convolution_bitcast_fusion.4 = f32[64,4,1024]{2,0,1:T(8,128)S(1)} fusion(bf16[64,4,1024]{2,0,1:T(8,128)(2,1)S(1)} %fusion.13, bf16[4,1024,1024]{2,1,0:T(8,128)(2,1)} %all-gather.2.cloned.1.call-done), kind=kOutput, calls=%fused_computation.22 | convolution fusion | flops 536870912 | bytes 9961472 | tf_op jit(solution)/shard_map/sgm,gmn->sgn/dot_general | solution.py:82
  116.7 1.9 %copy.50 = f32[64,4,1024]{0,2,1:T(8,128)} copy(f32[64,4,1024]{2,0,1:T(8,128)S(1)} %convolution_bitcast_fusion.4) | data formatting | bytes 2097152 | tf_op jit(solution)/shard_map/sgm,gmn->sgn/transpose | solution.py:82
  118.6 1.5 gather_fusion.5
  120.2 2.7 %collective-permute-start.7 = (f32[64,64]{0,1:T(8,128)S(1)}, f32[64,64]{0,1:T(8,128)S(1)}, u32[]{:S(2)}, u32[]{:S(2)}) collective-permute-start(f32[64,64]{0,1:T(8,128)S(1)} %bitcast.171), channel_id=1, source_target_pairs={{0,4},{4,0},{8,12},{12,8},{16,20},{20,16},{24,28},{28,24},{1,5},{5... | collective-permute-start | bytes 49160 | tf_op jit(solution)/shard_map/ppermute | solution.py:89
  122.9 1.9 %collective-permute-done.7 = f32[64,64]{0,1:T(8,128)S(1)} collective-permute-done((f32[64,64]{0,1:T(8,128)S(1)}, f32[64,64]{0,1:T(8,128)S(1)}, u32[]{:S(2)}, u32[]{:S(2)}) %collective-permute-start.7) | collective-permute-done | bytes 16416 | tf_op jit(solution)/shard_map/ppermute | solution.py:89
  124.8 2.0 %collective-permute-start.8 = (f32[64,128]{0,1:T(8,128)S(1)}, f32[64,128]{0,1:T(8,128)S(1)}, u32[]{:S(2)}, u32[]{:S(2)}) collective-permute-start(f32[64,128]{0,1:T(8,128)S(1)} %maximum_select_fusion.10), channel_id=1, source_target_pairs={{0,8},{4,12},{8,0},{12,4},{16,24},{20,28},{24,16},{28,20},{1,9},{5... | collective-permute-start | bytes 98312 | tf_op jit(solution)/shard_map/ppermute | solution.py:89
  126.8 2.8 %collective-permute-done.8 = f32[64,128]{0,1:T(8,128)S(1)} collective-permute-done((f32[64,128]{0,1:T(8,128)S(1)}, f32[64,128]{0,1:T(8,128)S(1)}, u32[]{:S(2)}, u32[]{:S(2)}) %collective-permute-start.8) | collective-permute-done | bytes 32800 | tf_op jit(solution)/shard_map/ppermute | solution.py:89
  129.6 3.2 %collective-permute-start.9 = (f32[64,256]{0,1:T(8,128)S(1)}, f32[64,256]{0,1:T(8,128)S(1)}, u32[]{:S(2)}, u32[]{:S(2)}) collective-permute-start(f32[64,256]{0,1:T(8,128)S(1)} %maximum_select_fusion.7), channel_id=1, source_target_pairs={{0,16},{4,20},{8,24},{12,28},{16,0},{20,4},{24,8},{28,12},{1,17},{... | collective-permute-start | bytes 196616 | tf_op jit(solution)/shard_map/ppermute | solution.py:89
  133.4 0.6 broadcast_in_dim.288
  134.7 0.7 broadcast_in_dim.292
  135.3 0.7 broadcast_in_dim.294
  136.4 0.7 copy.51
  137.2 1.1 fusion.5
  138.3 2.8 %fusion.14 = bf16[64,4,1024]{2,0,1:T(8,128)(2,1)S(1)} fusion(f32[64,4,1024]{2,0,1:T(8,128)S(1)} %fusion.5, f32[64]{0:T(128)} %get-tuple-element.33, s32[4,1024]{1,0:T(4,128)} %copy-done.12, f32[4,1024]{1,0:T(4,128)S(1)} %copy-done.14, f32[4]{0:T(128)} %copy-done.18, s32[64]{0:T(128)} %param.22, f32[64,4,1024]{2,0,1:T(8,128)S(1)} %fusion.9, ...), kind=kOutput, calls=%fused_computation.35 | convolution fusion | flops 53596160 | bytes 3777936 | tf_op jit(solution)/shard_map/sgp,gpn->sgn/dot_general | solution.py:73
  141.2 5.0 %convolution_bitcast_fusion.1 = f32[64,4,1024]{2,0,1:T(8,128)S(1)} fusion(bf16[64,4,1024]{2,0,1:T(8,128)(2,1)S(1)} %fusion.14, bf16[4,1024,1024]{2,1,0:T(8,128)(2,1)} %all-gather.2.cloned.1.call-done), kind=kOutput, calls=%fused_computation.15 | convolution fusion | flops 536870912 | bytes 9961472 | tf_op jit(solution)/shard_map/sgm,gmn->sgn/dot_general | solution.py:82
  146.2 1.9 %copy.52 = f32[64,4,1024]{0,2,1:T(8,128)} copy(f32[64,4,1024]{2,0,1:T(8,128)S(1)} %convolution_bitcast_fusion.1) | data formatting | bytes 2097152 | tf_op jit(solution)/shard_map/sgm,gmn->sgn/transpose | solution.py:82
  148.1 1.5 gather_fusion.6
  149.7 3.1 %collective-permute-start.10 = (f32[64,64]{0,1:T(8,128)S(1)}, f32[64,64]{0,1:T(8,128)S(1)}, u32[]{:S(2)}, u32[]{:S(2)}) collective-permute-start(f32[64,64]{0,1:T(8,128)S(1)} %bitcast.169), channel_id=1, source_target_pairs={{0,4},{4,0},{8,12},{12,8},{16,20},{20,16},{24,28},{28,24},{1,5},{5... | collective-permute-start | bytes 49160 | tf_op jit(solution)/shard_map/ppermute | solution.py:89
  152.8 1.9 %collective-permute-done.10 = f32[64,64]{0,1:T(8,128)S(1)} collective-permute-done((f32[64,64]{0,1:T(8,128)S(1)}, f32[64,64]{0,1:T(8,128)S(1)}, u32[]{:S(2)}, u32[]{:S(2)}) %collective-permute-start.10) | collective-permute-done | bytes 16416 | tf_op jit(solution)/shard_map/ppermute | solution.py:89
  154.7 1.5 collective-permute-start.11
  156.2 2.8 %collective-permute-done.11 = f32[64,128]{0,1:T(8,128)S(1)} collective-permute-done((f32[64,128]{0,1:T(8,128)S(1)}, f32[64,128]{0,1:T(8,128)S(1)}, u32[]{:S(2)}, u32[]{:S(2)}) %collective-permute-start.11) | collective-permute-done | bytes 32800 | tf_op jit(solution)/shard_map/ppermute | solution.py:89
  159.1 2.5 %collective-permute-start.12 = (f32[64,256]{0,1:T(8,128)S(1)}, f32[64,256]{0,1:T(8,128)S(1)}, u32[]{:S(2)}, u32[]{:S(2)}) collective-permute-start(f32[64,256]{0,1:T(8,128)S(1)} %maximum_select_fusion.8), channel_id=1, source_target_pairs={{0,16},{4,20},{8,24},{12,28},{16,0},{20,4},{24,8},{28,12},{1,17},{... | collective-permute-start | bytes 196616 | tf_op jit(solution)/shard_map/ppermute | solution.py:89
  161.6 0.7 multiply_convert_fusion.2
  162.3 1.9 %copy.54 = f32[64,4,1024]{0,2,1:T(8,128)} copy(f32[64,4,1024]{2,0,1:T(8,128)S(1)} %fusion.5) | data formatting | bytes 2097152 | tf_op jit(solution)/shard_map/mul | solution.py:107
  164.2 1.5 gather_fusion.7
  165.7 0.7 collective-permute-done.12
  166.9 1.1 fusion.121
  168.7 0.9 gather_fusion.8
  169.7 1.7 multiply_convert_fusion.1
  171.4 1.7 multiply_convert_fusion
  173.3 0.7 copy.59
  174.0 1.2 copy.58
  (154 shorter events, 6.9 us)
Async XLA Ops:
  7.2 87.7 %copy-start = (bf16[64,512]{1,0:T(8,128)(2,1)S(1)}, bf16[64,512]{1,0:T(8,128)(2,1)}, u32[]{:S(2)}) copy-start(bf16[64,512]{1,0:T(8,128)(2,1)} %param.14) | copy-start | bytes 196612
  7.2 7.8 %copy-start.51 = (s32[64]{0:T(128)S(1)}, s32[64]{0:T(128)}, u32[]{:S(2)}) copy-start(s32[64]{0:T(128)} %param.17) | copy-start | bytes 772
  7.2 7.8 %copy-start.52 = (s32[64]{0:T(128)S(1)}, s32[64]{0:T(128)}, u32[]{:S(2)}) copy-start(s32[64]{0:T(128)} %param.18) | copy-start | bytes 772
  7.2 8.5 %copy-start.50 = (f32[64]{0:T(128)S(1)}, f32[64]{0:T(128)}, u32[]{:S(2)}) copy-start(f32[64]{0:T(128)} %param.23) | copy-start | bytes 772
  7.2 9.1 %copy-start.16 = (s32[4,16]{1,0:T(4,128)S(1)}, s32[4,16]{1,0:T(4,128)}, u32[]{:S(2)}) copy-start(s32[4,16]{1,0:T(4,128)} %param.15) | copy-start | bytes 772
  7.2 13.1 %copy-start.2 = (f32[64,4,1024]{2,1,0:T(4,128)S(1)}, f32[64,4,1024]{2,1,0:T(4,128)}, u32[]{:S(2)}) copy-start(f32[64,4,1024]{2,1,0:T(4,128)} %param.20) | copy-start | bytes 3145732
  7.2 13.1 %copy-start.42 = (s32[64]{0:T(128)S(1)}, s32[64]{0:T(128)}, u32[]{:S(2)}) copy-start(s32[64]{0:T(128)} %param.22) | copy-start | bytes 772
  7.3 63.4 %all-gather.2.cloned.1.call-start = ((), (), s32[]{:S(2)}) async-start(), calls=%async_computation | async-start | bytes 10485760 | tf_op jit(solution)/shard_map/all_gather | solution.py:57
  8.2 8.8 %collective-permute-start = (bf16[4,64,64]{1,0,2:T(4,128)(2,1)S(1)}, bf16[4,64,64]{1,0,2:T(4,128)(2,1)S(1)}, u32[]{:S(2)}, u32[]{:S(2)}) collective-permute-start(bf16[4,64,64]{1,0,2:T(4,128)(2,1)S(1)} %copy.44), channel_id=1, source_target_pairs={{0,4},{4,8},{8,12},{12,16},{16,20},{20,24},{24,28},{1,5},{5,9},{9,... | collective-permute-start | bytes 98312 | tf_op jit(solution)/shard_map/ppermute | solution.py:15
  13.0 6.2 %collective-permute-start.1 = (bf16[4,64,64]{1,0,2:T(4,128)(2,1)S(1)}, bf16[4,64,64]{1,0,2:T(4,128)(2,1)S(1)}, u32[]{:S(2)}, u32[]{:S(2)}) collective-permute-start(bf16[4,64,64]{1,0,2:T(4,128)(2,1)S(1)} %copy.44), channel_id=1, source_target_pairs={{4,0},{8,4},{12,8},{16,12},{20,16},{24,20},{28,24},{5,1},{9,5},{13... | collective-permute-start | bytes 98312 | tf_op jit(solution)/shard_map/ppermute | solution.py:18
  15.6 1.2 copy-start.26
  15.6 60.0 %copy-start.20 = (pred[64]{0:T(512)(128)(4,1)}, pred[64]{0:T(512)(128)(4,1)S(1)}, u32[]{:S(2)}) copy-start(pred[64]{0:T(512)(128)(4,1)S(1)} %get-tuple-element.9) | copy-start | bytes 196
  15.6 60.0 %copy-start.28 = (pred[64]{0:T(512)(128)(4,1)}, pred[64]{0:T(512)(128)(4,1)S(1)}, u32[]{:S(2)}) copy-start(pred[64]{0:T(512)(128)(4,1)S(1)} %get-tuple-element.41) | copy-start | bytes 196
  15.6 60.1 %copy-start.30 = (pred[64]{0:T(512)(128)(4,1)}, pred[64]{0:T(512)(128)(4,1)S(1)}, u32[]{:S(2)}) copy-start(pred[64]{0:T(512)(128)(4,1)S(1)} %get-tuple-element.42) | copy-start | bytes 196
  15.7 60.1 %copy-start.32 = (pred[64]{0:T(512)(128)(4,1)}, pred[64]{0:T(512)(128)(4,1)S(1)}, u32[]{:S(2)}) copy-start(pred[64]{0:T(512)(128)(4,1)S(1)} %get-tuple-element.43) | copy-start | bytes 196
  15.7 60.0 %copy-start.25 = (s32[1024]{0:T(1024)}, s32[1024]{0:T(1024)S(1)}, u32[]{:S(2)}) copy-start(s32[1024]{0:T(1024)S(1)} %pad_clamp_fusion) | copy-start | bytes 12292
  16.4 59.3 %copy-start.12 = (s32[4,1024]{1,0:T(4,128)}, s32[4,1024]{1,0:T(4,128)S(1)}, u32[]{:S(2)}) copy-start(s32[4,1024]{1,0:T(4,128)S(1)} %iota_add_fusion) | copy-start | bytes 49156
  16.4 79.0 %copy-start.18 = (f32[4]{0:T(128)}, f32[4]{0:T(128)S(1)}, u32[]{:S(2)}) copy-start(f32[4]{0:T(128)S(1)} %compare_convert_fusion.1) | copy-start | bytes 52
  16.5 59.2 %copy-start.22 = (f32[4,16]{1,0:T(4,128)}, f32[4,16]{1,0:T(4,128)S(1)}, u32[]{:S(2)}) copy-start(f32[4,16]{1,0:T(4,128)S(1)} %mul.238) | copy-start | bytes 772
  20.3 55.5 %copy-start.3 = (f32[1,64,64]{1,0,2:T(1,128)}, f32[1,64,64]{1,0,2:T(1,128)S(1)}, u32[]{:S(2)}) copy-start(f32[1,64,64]{1,0,2:T(1,128)S(1)} %get-tuple-element.12) | copy-start | bytes 49156
  20.3 55.5 %copy-start.5 = (f32[1,64,64]{1,0,2:T(1,128)}, f32[1,64,64]{1,0,2:T(1,128)S(1)}, u32[]{:S(2)}) copy-start(f32[1,64,64]{1,0,2:T(1,128)S(1)} %get-tuple-element.13) | copy-start | bytes 49156
  20.3 55.5 %copy-start.6 = (f32[1,64,64]{1,0,2:T(1,128)}, f32[1,64,64]{1,0,2:T(1,128)S(1)}, u32[]{:S(2)}) copy-start(f32[1,64,64]{1,0,2:T(1,128)S(1)} %get-tuple-element.14) | copy-start | bytes 49156
  79.3 4.0 %collective-permute-start.2 = (f32[64,64]{0,1:T(8,128)S(1)}, f32[64,64]{0,1:T(8,128)S(1)}, u32[]{:S(2)}, u32[]{:S(2)}) collective-permute-start(f32[64,64]{0,1:T(8,128)S(1)} %bitcast.167), channel_id=1, source_target_pairs={{0,4},{4,0},{8,12},{12,8},{16,20},{20,16},{24,28},{28,24},{1,5},{5... | collective-permute-start | bytes 49160 | tf_op jit(solution)/shard_map/ppermute | solution.py:89
  83.2 4.3 %collective-permute-start.3 = (f32[64,128]{0,1:T(8,128)S(1)}, f32[64,128]{0,1:T(8,128)S(1)}, u32[]{:S(2)}, u32[]{:S(2)}) collective-permute-start(f32[64,128]{0,1:T(8,128)S(1)} %maximum_select_fusion.9), channel_id=1, source_target_pairs={{0,8},{4,12},{8,0},{12,4},{16,24},{20,28},{24,16},{28,20},{1,9},{5... | collective-permute-start | bytes 98312 | tf_op jit(solution)/shard_map/ppermute | solution.py:89
  87.6 7.3 %collective-permute-start.4 = (f32[64,256]{0,1:T(8,128)S(1)}, f32[64,256]{0,1:T(8,128)S(1)}, u32[]{:S(2)}, u32[]{:S(2)}) collective-permute-start(f32[64,256]{0,1:T(8,128)S(1)} %maximum_select_fusion.6), channel_id=1, source_target_pairs={{0,16},{4,20},{8,24},{12,28},{16,0},{20,4},{24,8},{28,12},{1,17},{... | collective-permute-start | bytes 196616 | tf_op jit(solution)/shard_map/ppermute | solution.py:89
  90.1 5.4 %copy-start.23 = (pred[4,16]{1,0:T(4,128)(4,1)}, pred[4,16]{1,0:T(4,128)(4,1)S(1)}, u32[]{:S(2)}) copy-start(pred[4,16]{1,0:T(4,128)(4,1)S(1)} %compare_and_fusion) | copy-start | bytes 196
  97.3 10.7 %copy-start.7 = (f32[64,4,16]{0,2,1:T(8,128)}, f32[64,4,16]{0,2,1:T(8,128)S(1)}, u32[]{:S(2)}) copy-start(f32[64,4,16]{0,2,1:T(8,128)S(1)} %bitcast_multiply_fusion.2) | copy-start | bytes 49156
  98.3 9.8 %collective-permute-start.5 = (bf16[64,64]{0,1:T(8,128)(2,1)S(1)}, bf16[64,64]{0,1:T(8,128)(2,1)S(1)}, u32[]{:S(2)}, u32[]{:S(2)}) collective-permute-start(bf16[64,64]{0,1:T(8,128)(2,1)S(1)} %fusion.63), channel_id=1, source_target_pairs={{0,4},{4,8},{8,12},{12,16},{16,20},{20,24},{24,28},{1,5},{5,9},{9,... | collective-permute-start | bytes 24584 | tf_op jit(solution)/shard_map/ppermute | solution.py:15
  101.7 6.4 %collective-permute-start.6 = (bf16[64,64]{0,1:T(8,128)(2,1)S(1)}, bf16[64,64]{0,1:T(8,128)(2,1)S(1)}, u32[]{:S(2)}, u32[]{:S(2)}) collective-permute-start(bf16[64,64]{0,1:T(8,128)(2,1)S(1)} %fusion.63), channel_id=1, source_target_pairs={{4,0},{8,4},{12,8},{16,12},{20,16},{24,20},{28,24},{5,1},{9,5},{13... | collective-permute-start | bytes 24584 | tf_op jit(solution)/shard_map/ppermute | solution.py:18
  103.9 12.7 %copy-start.13 = (f32[4,1024]{1,0:T(4,128)}, f32[4,1024]{1,0:T(4,128)S(1)}, u32[]{:S(2)}) copy-start(f32[4,1024]{1,0:T(4,128)S(1)} %broadcast_multiply_fusion) | copy-start | bytes 49156
  104.6 12.0 %copy-start.43 = (pred[4,16]{1,0:T(4,128)(4,1)}, pred[4,16]{1,0:T(4,128)(4,1)S(1)}, u32[]{:S(2)}) copy-start(pred[4,16]{1,0:T(4,128)(4,1)S(1)} %broadcast_in_dim.277) | copy-start | bytes 196
  108.9 7.8 %copy-start.9 = (bf16[64,64]{1,0:T(8,128)(2,1)}, bf16[64,64]{1,0:T(8,128)(2,1)S(1)}, u32[]{:S(2)}) copy-start(bf16[64,64]{1,0:T(8,128)(2,1)S(1)} %gather_fusion.1) | copy-start | bytes 24580
  116.7 16.1 %copy-start.41 = (pred[64]{0:T(512)(128)(4,1)S(1)}, pred[64]{0:T(512)(128)(4,1)}, u32[]{:S(2)}) copy-start(pred[64]{0:T(512)(128)(4,1)} %get-tuple-element.52) | copy-start | bytes 196
  116.7 16.8 %copy-start.40 = (pred[64]{0:T(512)(128)(4,1)S(1)}, pred[64]{0:T(512)(128)(4,1)}, u32[]{:S(2)}) copy-start(pred[64]{0:T(512)(128)(4,1)} %get-tuple-element.51) | copy-start | bytes 196
  116.7 17.4 %copy-start.38 = (pred[64]{0:T(512)(128)(4,1)S(1)}, pred[64]{0:T(512)(128)(4,1)}, u32[]{:S(2)}) copy-start(pred[64]{0:T(512)(128)(4,1)} %get-tuple-element.50) | copy-start | bytes 196
  116.7 18.0 %copy-start.36 = (pred[64]{0:T(512)(128)(4,1)S(1)}, pred[64]{0:T(512)(128)(4,1)}, u32[]{:S(2)}) copy-start(pred[64]{0:T(512)(128)(4,1)} %get-tuple-element.49) | copy-start | bytes 196
  116.7 18.7 %copy-start.34 = (pred[64]{0:T(512)(128)(4,1)S(1)}, pred[64]{0:T(512)(128)(4,1)}, u32[]{:S(2)}) copy-start(pred[64]{0:T(512)(128)(4,1)} %get-tuple-element.48) | copy-start | bytes 196
  118.6 19.6 %copy-start.4 = (f32[1,64,64]{1,0,2:T(1,128)S(1)}, f32[1,64,64]{1,0,2:T(1,128)}, u32[]{:S(2)}) copy-start(f32[1,64,64]{1,0,2:T(1,128)} %copy-done.3) | copy-start | bytes 49156
  120.2 4.6 %collective-permute-start.7 = (f32[64,64]{0,1:T(8,128)S(1)}, f32[64,64]{0,1:T(8,128)S(1)}, u32[]{:S(2)}, u32[]{:S(2)}) collective-permute-start(f32[64,64]{0,1:T(8,128)S(1)} %bitcast.171), channel_id=1, source_target_pairs={{0,4},{4,0},{8,12},{12,8},{16,20},{20,16},{24,28},{28,24},{1,5},{5... | collective-permute-start | bytes 49160 | tf_op jit(solution)/shard_map/ppermute | solution.py:89
  124.8 4.8 %collective-permute-start.8 = (f32[64,128]{0,1:T(8,128)S(1)}, f32[64,128]{0,1:T(8,128)S(1)}, u32[]{:S(2)}, u32[]{:S(2)}) collective-permute-start(f32[64,128]{0,1:T(8,128)S(1)} %maximum_select_fusion.10), channel_id=1, source_target_pairs={{0,8},{4,12},{8,0},{12,4},{16,24},{20,28},{24,16},{28,20},{1,9},{5... | collective-permute-start | bytes 98312 | tf_op jit(solution)/shard_map/ppermute | solution.py:89
  129.6 6.5 %collective-permute-start.9 = (f32[64,256]{0,1:T(8,128)S(1)}, f32[64,256]{0,1:T(8,128)S(1)}, u32[]{:S(2)}, u32[]{:S(2)}) collective-permute-start(f32[64,256]{0,1:T(8,128)S(1)} %maximum_select_fusion.7), channel_id=1, source_target_pairs={{0,16},{4,20},{8,24},{12,28},{16,0},{20,4},{24,8},{28,12},{1,17},{... | collective-permute-start | bytes 196616 | tf_op jit(solution)/shard_map/ppermute | solution.py:89
  137.1 1.2 copy-start.44
  137.1 1.2 copy-start.45
  137.1 1.2 copy-start.46
  137.1 1.2 copy-start.47
  137.1 1.2 copy-start.48
  137.2 1.2 copy-start.49
  146.2 15.4 %copy-start.8 = (f32[64,4,16]{0,2,1:T(8,128)S(1)}, f32[64,4,16]{0,2,1:T(8,128)}, u32[]{:S(2)}) copy-start(f32[64,4,16]{0,2,1:T(8,128)} %copy-done.7) | copy-start | bytes 49156
  146.2 15.4 %copy-start.17 = (f32[64]{0:T(128)S(1)}, f32[64]{0:T(128)}, u32[]{:S(2)}) copy-start(f32[64]{0:T(128)} %mul.248) | copy-start | bytes 772
  146.2 15.4 %copy-start.27 = (pred[64]{0:T(512)(128)(4,1)S(1)}, pred[64]{0:T(512)(128)(4,1)}, u32[]{:S(2)}) copy-start(pred[64]{0:T(512)(128)(4,1)} %copy-done.26) | copy-start | bytes 196
  146.2 15.4 %copy-start.29 = (pred[64]{0:T(512)(128)(4,1)S(1)}, pred[64]{0:T(512)(128)(4,1)}, u32[]{:S(2)}) copy-start(pred[64]{0:T(512)(128)(4,1)} %copy-done.28) | copy-start | bytes 196
  146.2 15.4 %copy-start.31 = (pred[64]{0:T(512)(128)(4,1)S(1)}, pred[64]{0:T(512)(128)(4,1)}, u32[]{:S(2)}) copy-start(pred[64]{0:T(512)(128)(4,1)} %copy-done.30) | copy-start | bytes 196
  146.2 15.4 %copy-start.33 = (pred[64]{0:T(512)(128)(4,1)S(1)}, pred[64]{0:T(512)(128)(4,1)}, u32[]{:S(2)}) copy-start(pred[64]{0:T(512)(128)(4,1)} %copy-done.32) | copy-start | bytes 196
  149.7 5.0 %collective-permute-start.10 = (f32[64,64]{0,1:T(8,128)S(1)}, f32[64,64]{0,1:T(8,128)S(1)}, u32[]{:S(2)}, u32[]{:S(2)}) collective-permute-start(f32[64,64]{0,1:T(8,128)S(1)} %bitcast.169), channel_id=1, source_target_pairs={{0,4},{4,0},{8,12},{12,8},{16,20},{20,16},{24,28},{28,24},{1,5},{5... | collective-permute-start | bytes 49160 | tf_op jit(solution)/shard_map/ppermute | solution.py:89
  154.7 4.3 %collective-permute-start.11 = (f32[64,128]{0,1:T(8,128)S(1)}, f32[64,128]{0,1:T(8,128)S(1)}, u32[]{:S(2)}, u32[]{:S(2)}) collective-permute-start(f32[64,128]{0,1:T(8,128)S(1)} %maximum_select_fusion.11), channel_id=1, source_target_pairs={{0,8},{4,12},{8,0},{12,4},{16,24},{20,28},{24,16},{28,20},{1,9},{5... | collective-permute-start | bytes 98312 | tf_op jit(solution)/shard_map/ppermute | solution.py:89
  159.1 7.3 %collective-permute-start.12 = (f32[64,256]{0,1:T(8,128)S(1)}, f32[64,256]{0,1:T(8,128)S(1)}, u32[]{:S(2)}, u32[]{:S(2)}) collective-permute-start(f32[64,256]{0,1:T(8,128)S(1)} %maximum_select_fusion.8), channel_id=1, source_target_pairs={{0,16},{4,20},{8,24},{12,28},{16,0},{20,4},{24,8},{28,12},{1,17},{... | collective-permute-start | bytes 196616 | tf_op jit(solution)/shard_map/ppermute | solution.py:89
  162.3 4.6 %copy-start.19 = (f32[4]{0:T(128)S(1)}, f32[4]{0:T(128)}, u32[]{:S(2)}) copy-start(f32[4]{0:T(128)} %copy-done.18) | copy-start | bytes 52
  162.3 4.6 %copy-start.24 = (pred[4,16]{1,0:T(4,128)(4,1)S(1)}, pred[4,16]{1,0:T(4,128)(4,1)}, u32[]{:S(2)}) copy-start(pred[4,16]{1,0:T(4,128)(4,1)} %copy-done.23) | copy-start | bytes 196
  168.1 1.6 copy-start.11
  168.1 1.6 copy-start.21
  168.1 3.3 %copy-start.35 = (pred[64]{0:T(512)(128)(4,1)S(1)}, pred[64]{0:T(512)(128)(4,1)}, u32[]{:S(2)}) copy-start(pred[64]{0:T(512)(128)(4,1)} %get-tuple-element.48) | copy-start | bytes 196
  168.1 3.3 %copy-start.37 = (pred[64]{0:T(512)(128)(4,1)S(1)}, pred[64]{0:T(512)(128)(4,1)}, u32[]{:S(2)}) copy-start(pred[64]{0:T(512)(128)(4,1)} %get-tuple-element.49) | copy-start | bytes 196
  168.1 3.3 %copy-start.39 = (pred[64]{0:T(512)(128)(4,1)S(1)}, pred[64]{0:T(512)(128)(4,1)}, u32[]{:S(2)}) copy-start(pred[64]{0:T(512)(128)(4,1)} %get-tuple-element.50) | copy-start | bytes 196
  168.7 5.3 %copy-start.1 = (bf16[64,4,1024]{2,0,1:T(8,128)(2,1)S(1)}, bf16[64,4,1024]{2,0,1:T(8,128)(2,1)}, u32[]{:S(2)}) copy-start(bf16[64,4,1024]{2,0,1:T(8,128)(2,1)} %get-tuple-element.37) | copy-start | bytes 1572868
  (3 other events, 3.1 us)
Sparse Core Ops, SparseCore 0:
  9.7 60.9 all-gather.1
